TPU v7x, 32 devices: a whole 2x2x4 slice. The times are simulated.
32 devices in a mesh: tiles: 1, rows: 32 (over z, y, x, core).
Axes of the slice: x: 2, y: 2, z: 4, core: 2. Of those that a mesh axis runs over, the one named last changes fastest.
Arguments:
- features: bfloat16 [512, 512, 256], P(('tiles', 'rows')), may hold values from -6 to 6
- corners: int32 [256, 2], P(('tiles', 'rows')), may hold values from 0 to 511, as said below
- offsets: int32 [256, 1], P(('tiles', 'rows')), may hold values from 0 to 3; in each aligned block of 8 rows (0 to 7, 8 to 15, ...) at most 2 rows name the same one
- counts: int32 [32], P(('tiles', 'rows')), may hold values from 4 to 8, as said below
- classes: int32 [256], P(('tiles', 'rows')), may hold values from 0 to 14
- fpn_weight: bfloat16 [2304, 256], replicated, may hold values from -0.125 to 0.125
- head_weight: bfloat16 [2304, 256], replicated, may hold values from -0.125 to 0.125
- deconv_weight: bfloat16 [256, 1024], replicated, may hold values from -0.375 to 0.375
- class_weight: bfloat16 [15, 256], replicated, may hold values from -0.375 to 0.375
Outputs:
- masks: float32 [256, 1024], P(('tiles', 'rows'))
Inputs may be any that keep to these rules, and one draw needn't show every extreme that they name: corners[q, 0] lies in owner q // 8's band of rows 16 (q // 8) .. 16 (q // 8 + 1) - 1; corners[q, 1] is at most 496. `offsets`: in each owner's 8 slots no offset occurs more than 2 times, and some offset occurs exactly 2 times. `counts`: some owner has all 8 slots live.
All inputs are finite; a program needn't handle non-finite values.
Results may differ from a plain program's by a relative error of at most 0.0051.
Values may be sent and summed in bfloat16 or wider, within the bound.
A program may use at most 192 MiB of HBM per device.

v0:
```python
import jax
import jax.numpy as jnp
from jax import lax
from jax.sharding import PartitionSpec as P

ROI_SIZE = 16
WINDOW = 4
SLOTS = 2


def extended(cells, sides, width):
    for axis, dim in sides:
        count = lax.axis_size(axis)
        ends = count - 1
        head = lax.slice_in_dim(cells, 0, width, axis=dim)
        tail = lax.slice_in_dim(cells, cells.shape[dim] - width, cells.shape[dim], axis=dim)
        cells = jnp.concatenate(
            [
                lax.ppermute(tail, axis, [(i, (i + 1) % count) for i in range(ends)]),
                cells,
                lax.ppermute(head, axis, [((i + 1) % count, i) for i in range(ends)]),
            ],
            axis=dim,
        )
    return cells


def passed_along(x, axis, by):
    devices = lax.axis_size(axis)
    pairs = [(i, i + by) for i in range(devices) if 0 <= i + by < devices]
    return lax.ppermute(x, axis, pairs)


def passed_along_2(block, axis, distance):
    devices = range(lax.axis_size(axis))
    route = [((i - distance) % len(devices), i) for i in devices]
    return lax.ppermute(block, axis, route)


def conv_taps(padded, weights):
    chans = padded.shape[-1]
    height = padded.shape[-3] - 2
    width = padded.shape[-2] - 2
    total = None
    for tap in range(9):
        row_off = tap // 3
        col_off = tap % 3
        window = padded[..., row_off : row_off + height, col_off : col_off + width, :]
        piece = weights[tap * chans : (tap + 1) * chans]
        term = jnp.einsum("...c,cd->...d", window, piece, preferred_element_type=jnp.float32)
        total = term if total is None else total + term
    return total


def mask_head(blocks, class_ids, head_weight, deconv_weight, class_weight):
    count, side, _, chans = blocks.shape
    padded = jnp.pad(blocks, ((0, 0), (1, 1), (1, 1), (0, 0)))
    hidden = jax.nn.relu(conv_taps(padded, head_weight)).astype(jnp.bfloat16)
    upsampled = jnp.einsum(
        "bhwc,ck->bhwk", hidden, deconv_weight, preferred_element_type=jnp.float32
    )
    upsampled = jax.nn.relu(upsampled).astype(jnp.bfloat16).reshape(count, side, side, 2, 2, chans)
    one_hot = (
        class_ids[:, None] == jnp.arange(class_weight.shape[0], dtype=jnp.int32)[None, :]
    ).astype(jnp.bfloat16)
    chosen = jnp.dot(one_hot, class_weight, preferred_element_type=jnp.float32).astype(jnp.bfloat16)
    logit = jnp.einsum("bhwyxc,bc->bhwyx", upsampled, chosen, preferred_element_type=jnp.float32)
    return logit.transpose(0, 1, 3, 2, 4).reshape(count, 4 * side * side)


def body(
    features,
    corners,
    offsets,
    counts,
    classes,
    fpn_weight,
    head_weight,
    deconv_weight,
    class_weight,
):
    band_rows, columns, chans = features.shape
    roi_dev = corners.shape[0]
    slot_total = WINDOW * SLOTS
    padded = extended(features, (("rows", 0),), 1)
    padded = jnp.pad(padded, ((0, 0), (1, 1), (0, 0)))
    fpn_band = conv_taps(padded, fpn_weight).astype(jnp.bfloat16)
    position = lax.axis_index("rows")
    tops = corners[:, 0] - position * band_rows
    lefts = corners[:, 1]
    below = passed_along(fpn_band[: ROI_SIZE - 1], "rows", -1)
    stacked = jnp.concatenate([fpn_band, below], 0)

    def crop(row_at, col_at):
        return lax.dynamic_slice(
            stacked, (row_at, col_at, jnp.int32(0)), (ROI_SIZE, ROI_SIZE, chans)
        )

    blocks = jax.vmap(crop)(tops, lefts)
    ordinal = jnp.arange(roi_dev, dtype=jnp.int32)
    valid = ordinal < counts[0]
    target = offsets[:, 0]
    earlier = (
        (target[:, None] == target[None, :])
        & valid[None, :]
        & (ordinal[None, :] < ordinal[:, None])
    )
    rank = jnp.sum(earlier.astype(jnp.int32), 1)
    slot_of = jnp.where(valid, target * SLOTS + rank, slot_total)
    select = jnp.arange(slot_total, dtype=jnp.int32)[:, None] == slot_of[None, :]
    outgoing = jnp.einsum(
        "qj,jhwc->qhwc", select.astype(jnp.bfloat16), blocks, preferred_element_type=jnp.float32
    ).astype(jnp.bfloat16)
    out_class = jnp.sum(select.astype(jnp.int32) * classes[None, :], 1)
    outgoing = outgoing.reshape(WINDOW, SLOTS, ROI_SIZE, ROI_SIZE, chans)
    out_class = out_class.reshape(WINDOW, SLOTS)
    arrived = [outgoing[0]]
    arrived_class = [out_class[0]]
    for offset_step in range(1, WINDOW):
        got_blocks, got_class = passed_along_2(
            (outgoing[offset_step], out_class[offset_step]), "rows", offset_step
        )
        arrived.append(got_blocks)
        arrived_class.append(got_class)
    incoming = jnp.stack(arrived, 0)
    incoming_class = jnp.stack(arrived_class, 0)
    masks = mask_head(
        incoming.reshape(slot_total, ROI_SIZE, ROI_SIZE, chans),
        incoming_class.reshape(slot_total),
        head_weight,
        deconv_weight,
        class_weight,
    )
    return masks


def solution(mesh):
    placed = (
        P(("tiles", "rows"), None, None),
        P(("tiles", "rows"), None),
        P(("tiles", "rows"), None),
        P(("tiles", "rows")),
        P(("tiles", "rows")),
        P(),
        P(),
        P(),
        P(),
    )
    return jax.shard_map(
        body, mesh=mesh, in_specs=placed, out_specs=P(("tiles", "rows"), None), check_vma=False
    )
```

profile of v0, /device:TPU:8, one launch (start us, length us, event | category | flops | bytes accessed | tf_op | source)
XLA Modules:
  0.0 227.1 jit_solution(7102189366079096625)
XLA Ops:
  1.1 1.9 collective-permute-start
  3.1 5.7 %collective-permute-start.1 = (bf16[1,512,256]{2,1,0:T(8,128)(2,1)S(1)}, bf16[1,512,256]{2,1,0:T(8,128)(2,1)S(1)}, u32[]{:S(2)}, u32[]{:S(2)}) collective-permute-start(bf16[1,512,256]{2,1,0:T(8,128)(2,1)S(1)} %get-tuple-element.24), channel_id=1, source_target_pairs={{1,0},{2,1},{3,2},{4,3},{5,4},{6,5},{7,6},{8,7},{9,8},{10,9},{11,1... | collective-permute-start | bytes 786440 | tf_op jit(solution)/shard_map/ppermute | solution.py:21
  8.8 6.8 %fusion.56 = f32[16,512,256]{2,1,0:T(8,128)} fusion(bf16[16,512,256]{2,1,0:T(8,128)(2,1)} %param.9, bf16[2304,256]{1,0:T(8,128)(2,1)} %param.14), kind=kOutput, calls=%fused_computation.73 | convolution fusion | flops 1073741824 | bytes 12713984 | tf_op jit(solution)/shard_map/...c,cd->...d/dot_general | solution.py:50
  15.6 2.9 %fusion.5 = bf16[18,514,256]{2,1,0:T(8,128)(2,1)S(1)} fusion(bf16[1,512,256]{2,1,0:T(8,128)(2,1)S(1)} %collective-permute-done.1, bf16[16,512,256]{2,1,0:T(8,128)(2,1)S(1)} %copy-done.2, bf16[1,512,256]{2,1,0:T(8,128)(2,1)S(1)} %collective-permute-done), kind=kLoop, calls=%fused_computation.12 | loop fusion | flops 28422144 | bytes 9455616 | tf_op jit(solution)/shard_map/concatenate | solution.py:17
  18.6 4.7 %fusion.16 = f32[16,512,256]{2,1,0:T(8,128)} fusion(bf16[18,514,256]{2,1,0:T(8,128)(2,1)S(1)} %fusion.5, bf16[2304,256]{1,0:T(8,128)(2,1)S(1)} %copy-done.3), kind=kOutput, calls=%fused_computation.23 | convolution fusion | flops 1073741824 | bytes 12713984 | tf_op jit(solution)/shard_map/...c,cd->...d/dot_general | solution.py:50
  23.3 4.5 %fusion.18 = f32[16,512,256]{2,1,0:T(8,128)} fusion(bf16[18,514,256]{2,1,0:T(8,128)(2,1)S(1)} %fusion.5, bf16[2304,256]{1,0:T(8,128)(2,1)S(1)} %copy-done.3), kind=kOutput, calls=%fused_computation.25 | convolution fusion | flops 1073741824 | bytes 12713984 | tf_op jit(solution)/shard_map/...c,cd->...d/dot_general | solution.py:50
  27.8 4.5 %fusion.20 = f32[16,512,256]{2,1,0:T(8,128)} fusion(bf16[18,514,256]{2,1,0:T(8,128)(2,1)S(1)} %fusion.5, bf16[2304,256]{1,0:T(8,128)(2,1)S(1)} %copy-done.3), kind=kOutput, calls=%fused_computation.27 | convolution fusion | flops 1073741824 | bytes 12713984 | tf_op jit(solution)/shard_map/...c,cd->...d/dot_general | solution.py:50
  32.3 4.6 %fusion.22 = f32[16,512,256]{2,1,0:T(8,128)} fusion(bf16[18,514,256]{2,1,0:T(8,128)(2,1)S(1)} %fusion.5, bf16[2304,256]{1,0:T(8,128)(2,1)S(1)} %copy-done.3), kind=kOutput, calls=%fused_computation.29 | convolution fusion | flops 1073741824 | bytes 12713984 | tf_op jit(solution)/shard_map/...c,cd->...d/dot_general | solution.py:50
  36.9 4.5 %fusion.24 = f32[16,512,256]{2,1,0:T(8,128)} fusion(bf16[18,514,256]{2,1,0:T(8,128)(2,1)S(1)} %fusion.5, bf16[2304,256]{1,0:T(8,128)(2,1)S(1)} %copy-done.3), kind=kOutput, calls=%fused_computation.31 | convolution fusion | flops 1073741824 | bytes 12713984 | tf_op jit(solution)/shard_map/...c,cd->...d/dot_general | solution.py:50
  41.3 4.5 %fusion.10 = f32[16,512,256]{2,1,0:T(8,128)} fusion(bf16[1,512,256]{2,1,0:T(8,128)(2,1)S(1)} %collective-permute-done.1, bf16[16,512,256]{2,1,0:T(8,128)(2,1)S(1)} %copy-done.2, bf16[2304,256]{1,0:T(8,128)(2,1)S(1)} %copy-done.3), kind=kOutput, calls=%fused_computation.17 | convolution fusion | flops 1082654720 | bytes 12976128 | tf_op jit(solution)/shard_map/...c,cd->...d/dot_general | solution.py:50
  45.8 4.5 %fusion.6 = f32[16,512,256]{2,1,0:T(8,128)} fusion(bf16[16,512,256]{2,1,0:T(8,128)(2,1)S(1)} %copy-done.2, bf16[1,512,256]{2,1,0:T(8,128)(2,1)S(1)} %collective-permute-done, bf16[2304,256]{1,0:T(8,128)(2,1)S(1)} %copy-done.3), kind=kOutput, calls=%fused_computation.13 | convolution fusion | flops 1082654720 | bytes 12976128 | tf_op jit(solution)/shard_map/...c,cd->...d/dot_general | solution.py:50
  50.4 25.0 %add_convert_fusion = bf16[16,512,256]{2,1,0:T(8,128)(2,1)} fusion(f32[16,512,256]{2,1,0:T(8,128)} %fusion.10, f32[16,512,256]{2,1,0:T(8,128)} %fusion.16, f32[16,512,256]{2,1,0:T(8,128)} %fusion.18, f32[16,512,256]{2,1,0:T(8,128)} %fusion.56, f32[16,512,256]{2,1,0:T(8,128)} %fusion.20, f32[16,512,256]{2,1,0:T(8,128)} %fusion.22, ...), kind=kOutput, calls=%fused_computation.6 | convolution fusion | flops 1092616192 | bytes 75628544 | tf_op jit(solution)/shard_map/...c,cd->...d/dot_general | solution.py:50
  75.4 4.4 %slice.230 = bf16[15,512,256]{2,1,0:T(8,128)(2,1)} slice(bf16[16,512,256]{2,1,0:T(8,128)(2,1)} %add_convert_fusion), slice={[0:15], [0:512], [0:256]} | slice | bytes 7864320 | tf_op jit(solution)/shard_map/slice | solution.py:91
  79.8 2.8 %collective-permute-start.2 = (bf16[15,512,256]{2,1,0:T(8,128)(2,1)}, bf16[15,512,256]{2,1,0:T(8,128)(2,1)}, u32[]{:S(2)}, u32[]{:S(2)}) collective-permute-start(bf16[15,512,256]{2,1,0:T(8,128)(2,1)} %slice.230), channel_id=1, source_target_pairs={{1,0},{2,1},{3,2},{4,3},{5,4},{6,5},{7,6},{8,7},{9,8},{10,9},{11,1... | collective-permute-start | bytes 11796488 | tf_op jit(solution)/shard_map/ppermute | solution.py:31
  83.7 42.3 %collective-permute-done.2 = bf16[15,512,256]{2,1,0:T(8,128)(2,1)} collective-permute-done((bf16[15,512,256]{2,1,0:T(8,128)(2,1)}, bf16[15,512,256]{2,1,0:T(8,128)(2,1)}, u32[]{:S(2)}, u32[]{:S(2)}) %collective-permute-start.2) | collective-permute-done | bytes 3932192 | tf_op jit(solution)/shard_map/ppermute | solution.py:31
  125.9 7.3 %pad_maximum_fusion = bf16[31,512,256]{2,1,0:T(8,128)(2,1)} fusion(bf16[15,512,256]{2,1,0:T(8,128)(2,1)} %collective-permute-done.2, bf16[16,512,256]{2,1,0:T(8,128)(2,1)} %add_convert_fusion), kind=kLoop, calls=%fused_computation.7 | loop fusion | flops 4063232 | bytes 16252928 | tf_op jit(solution)/shard_map/concatenate | solution.py:92
  133.2 24.4 %while.1 = (s32[]{:T(128)}, bf16[31,512,256]{2,1,0:T(8,128)(2,1)}, s32[8,3]{0,1:T(4,128)S(1)}, bf16[8,16,16,256]{3,2,1,0:T(8,128)(2,1)S(1)}, s32[]{:T(128)}) while((s32[]{:T(128)}, bf16[31,512,256]{2,1,0:T(8,128)(2,1)}, s32[8,3]{0,1:T(4,128)S(1)}, bf16[8,16,16,256]{3,2,1,0:T(8,128)(2,1)S(1)}, s32[]{:T(128)}) %tuple.27), condition=%wide.while_cond, body=%wide.while_body.sunk | while | flops 2 | bytes 262261 | solution.py:95
  133.9 2.4 %bitcast_dynamic-update-slice_fusion.2 = bf16[8,16,16,256]{3,2,1,0:T(8,128)(2,1)S(1)} fusion(bf16[8,16,16,256]{3,2,1,0:T(8,128)(2,1)S(1)} %get-tuple-element.72, s32[]{:T(128)} %get-tuple-element.69, bf16[31,512,256]{2,1,0:T(8,128)(2,1)} %get-tuple-element.75, s32[]{:T(128)} %bitcast.117, s32[]{:T(128)} %bitcast.118), kind=kLoop, calls=%fused_computation.clone.1 | loop fusion | bytes 262156 | tf_op jit(solution)/shard_map/vmap()/gather
  136.9 2.4 %bitcast_dynamic-update-slice_fusion.2 = bf16[8,16,16,256]{3,2,1,0:T(8,128)(2,1)S(1)} fusion(bf16[8,16,16,256]{3,2,1,0:T(8,128)(2,1)S(1)} %get-tuple-element.72, s32[]{:T(128)} %get-tuple-element.69, bf16[31,512,256]{2,1,0:T(8,128)(2,1)} %get-tuple-element.75, s32[]{:T(128)} %bitcast.117, s32[]{:T(128)} %bitcast.118), kind=kLoop, calls=%fused_computation.clone.1 | loop fusion | bytes 262156 | tf_op jit(solution)/shard_map/vmap()/gather
  140.0 2.4 %bitcast_dynamic-update-slice_fusion.2 = bf16[8,16,16,256]{3,2,1,0:T(8,128)(2,1)S(1)} fusion(bf16[8,16,16,256]{3,2,1,0:T(8,128)(2,1)S(1)} %get-tuple-element.72, s32[]{:T(128)} %get-tuple-element.69, bf16[31,512,256]{2,1,0:T(8,128)(2,1)} %get-tuple-element.75, s32[]{:T(128)} %bitcast.117, s32[]{:T(128)} %bitcast.118), kind=kLoop, calls=%fused_computation.clone.1 | loop fusion | bytes 262156 | tf_op jit(solution)/shard_map/vmap()/gather
  143.0 2.4 %bitcast_dynamic-update-slice_fusion.2 = bf16[8,16,16,256]{3,2,1,0:T(8,128)(2,1)S(1)} fusion(bf16[8,16,16,256]{3,2,1,0:T(8,128)(2,1)S(1)} %get-tuple-element.72, s32[]{:T(128)} %get-tuple-element.69, bf16[31,512,256]{2,1,0:T(8,128)(2,1)} %get-tuple-element.75, s32[]{:T(128)} %bitcast.117, s32[]{:T(128)} %bitcast.118), kind=kLoop, calls=%fused_computation.clone.1 | loop fusion | bytes 262156 | tf_op jit(solution)/shard_map/vmap()/gather
  146.1 2.4 %bitcast_dynamic-update-slice_fusion.2 = bf16[8,16,16,256]{3,2,1,0:T(8,128)(2,1)S(1)} fusion(bf16[8,16,16,256]{3,2,1,0:T(8,128)(2,1)S(1)} %get-tuple-element.72, s32[]{:T(128)} %get-tuple-element.69, bf16[31,512,256]{2,1,0:T(8,128)(2,1)} %get-tuple-element.75, s32[]{:T(128)} %bitcast.117, s32[]{:T(128)} %bitcast.118), kind=kLoop, calls=%fused_computation.clone.1 | loop fusion | bytes 262156 | tf_op jit(solution)/shard_map/vmap()/gather
  149.1 2.4 %bitcast_dynamic-update-slice_fusion.2 = bf16[8,16,16,256]{3,2,1,0:T(8,128)(2,1)S(1)} fusion(bf16[8,16,16,256]{3,2,1,0:T(8,128)(2,1)S(1)} %get-tuple-element.72, s32[]{:T(128)} %get-tuple-element.69, bf16[31,512,256]{2,1,0:T(8,128)(2,1)} %get-tuple-element.75, s32[]{:T(128)} %bitcast.117, s32[]{:T(128)} %bitcast.118), kind=kLoop, calls=%fused_computation.clone.1 | loop fusion | bytes 262156 | tf_op jit(solution)/shard_map/vmap()/gather
  152.2 2.4 %bitcast_dynamic-update-slice_fusion.2 = bf16[8,16,16,256]{3,2,1,0:T(8,128)(2,1)S(1)} fusion(bf16[8,16,16,256]{3,2,1,0:T(8,128)(2,1)S(1)} %get-tuple-element.72, s32[]{:T(128)} %get-tuple-element.69, bf16[31,512,256]{2,1,0:T(8,128)(2,1)} %get-tuple-element.75, s32[]{:T(128)} %bitcast.117, s32[]{:T(128)} %bitcast.118), kind=kLoop, calls=%fused_computation.clone.1 | loop fusion | bytes 262156 | tf_op jit(solution)/shard_map/vmap()/gather
  155.3 2.4 %bitcast_dynamic-update-slice_fusion.2 = bf16[8,16,16,256]{3,2,1,0:T(8,128)(2,1)S(1)} fusion(bf16[8,16,16,256]{3,2,1,0:T(8,128)(2,1)S(1)} %get-tuple-element.72, s32[]{:T(128)} %get-tuple-element.69, bf16[31,512,256]{2,1,0:T(8,128)(2,1)} %get-tuple-element.75, s32[]{:T(128)} %bitcast.117, s32[]{:T(128)} %bitcast.118), kind=kLoop, calls=%fused_computation.clone.1 | loop fusion | bytes 262156 | tf_op jit(solution)/shard_map/vmap()/gather
  161.3 3.2 %collective-permute-start.6 = (s32[2]{0:T(128)S(1)}, s32[2]{0:T(128)S(1)}, u32[]{:S(2)}, u32[]{:S(2)}) collective-permute-start(s32[2]{0:T(128)S(1)} %get-tuple-element.34), channel_id=1, source_target_pairs={{31,0},{0,1},{1,2},{2,3},{3,4},{4,5},{5,6},{6,7},{7,8},{8,9},{9,10... | collective-permute-start | bytes 32 | tf_op jit(solution)/shard_map/ppermute | solution.py:37
  165.3 16.0 %collective-permute-done.6 = s32[2]{0:T(128)S(1)} collective-permute-done((s32[2]{0:T(128)S(1)}, s32[2]{0:T(128)S(1)}, u32[]{:S(2)}, u32[]{:S(2)}) %collective-permute-start.6) | collective-permute-done | bytes 40 | tf_op jit(solution)/shard_map/ppermute | solution.py:37
  181.3 3.9 %collective-permute-done.8 = s32[2]{0:T(128)S(1)} collective-permute-done((s32[2]{0:T(128)S(1)}, s32[2]{0:T(128)S(1)}, u32[]{:S(2)}, u32[]{:S(2)}) %collective-permute-start.8) | collective-permute-done | bytes 40 | tf_op jit(solution)/shard_map/ppermute | solution.py:37
  185.5 2.0 pad_maximum_fusion.1
  201.9 9.0 %maximum_convert_fusion = bf16[8,16,16,1024]{3,2,1,0:T(8,128)(2,1)} fusion(f32[8,16,16,256]{3,2,1,0:T(8,128)} %fusion.37, f32[8,16,16,256]{3,2,1,0:T(8,128)} %fusion.36, f32[8,16,16,256]{3,2,1,0:T(8,128)} %fusion.35, f32[8,16,16,256]{3,2,1,0:T(8,128)} %fusion.46, f32[8,16,16,256]{3,2,1,0:T(8,128)} %fusion.34, f32[8,16,16,256]{3,2,1,0:T(8,128)} %fusion.33, ...), kind=kOutput, calls=%fused_computation.5 | convolution fusion | flops 1351614464 | bytes 22675456 | tf_op jit(solution)/shard_map/bhwc,ck->bhwk/dot_general | solution.py:59
  210.9 7.8 %reshape.44 = bf16[8,16,16,2,2,256]{5,4,3,2,1,0:T(2,128)(2,1)} reshape(bf16[8,16,16,1024]{3,2,1,0:T(8,128)(2,1)} %maximum_convert_fusion) | data formatting | bytes 8388608 | tf_op jit(solution)/shard_map/reshape | solution.py:62
  218.8 7.2 %fusion.26 = f32[8,1,16,16,2,2]{3,1,5,4,2,0:T(1,128)S(1)} fusion(bf16[8,16,16,2,2,256]{5,4,3,2,1,0:T(2,128)(2,1)} %reshape.44, bf16[8,256,1,1,1,1]{1,0,2,3,4,5:T(8,128)(2,1)S(1)} %fusion.30), kind=kOutput, calls=%fused_computation.33 | convolution fusion | flops 4194304 | bytes 4231168 | tf_op jit(solution)/shard_map/bhwyxc,bc->bhwyx/dot_general | solution.py:67
  (71 shorter events, 27.2 us)
Async XLA Ops:
  0.0 201.9 %copy-start = (bf16[256,1024]{1,0:T(8,128)(2,1)S(1)}, bf16[256,1024]{1,0:T(8,128)(2,1)}, u32[]{:S(2)}) copy-start(bf16[256,1024]{1,0:T(8,128)(2,1)} %param.16) | copy-start | bytes 1572868
  1.1 14.5 %collective-permute-start = (bf16[1,512,256]{2,1,0:T(8,128)(2,1)S(1)}, bf16[1,512,256]{2,1,0:T(8,128)(2,1)S(1)}, u32[]{:S(2)}, u32[]{:S(2)}) collective-permute-start(bf16[1,512,256]{2,1,0:T(8,128)(2,1)S(1)} %get-tuple-element.23), channel_id=1, source_target_pairs={{0,1},{1,2},{2,3},{3,4},{4,5},{5,6},{6,7},{7,8},{8,9},{9,10},{10,1... | collective-permute-start | bytes 786440 | tf_op jit(solution)/shard_map/ppermute | solution.py:19
  3.1 12.5 %copy-start.2 = (bf16[16,512,256]{2,1,0:T(8,128)(2,1)S(1)}, bf16[16,512,256]{2,1,0:T(8,128)(2,1)}, u32[]{:S(2)}) copy-start(bf16[16,512,256]{2,1,0:T(8,128)(2,1)} %param.9) | copy-start | bytes 12582916
  3.1 12.5 %collective-permute-start.1 = (bf16[1,512,256]{2,1,0:T(8,128)(2,1)S(1)}, bf16[1,512,256]{2,1,0:T(8,128)(2,1)S(1)}, u32[]{:S(2)}, u32[]{:S(2)}) collective-permute-start(bf16[1,512,256]{2,1,0:T(8,128)(2,1)S(1)} %get-tuple-element.24), channel_id=1, source_target_pairs={{1,0},{2,1},{3,2},{4,3},{5,4},{6,5},{7,6},{8,7},{9,8},{10,9},{11,1... | collective-permute-start | bytes 786440 | tf_op jit(solution)/shard_map/ppermute | solution.py:21
  15.6 3.0 %copy-start.3 = (bf16[2304,256]{1,0:T(8,128)(2,1)S(1)}, bf16[2304,256]{1,0:T(8,128)(2,1)}, u32[]{:S(2)}) copy-start(bf16[2304,256]{1,0:T(8,128)(2,1)} %param.14) | copy-start | bytes 3538948
  18.6 18.3 %copy-start.1 = (bf16[18,514,256]{2,1,0:T(8,128)(2,1)}, bf16[18,514,256]{2,1,0:T(8,128)(2,1)S(1)}, u32[]{:S(2)}) copy-start(bf16[18,514,256]{2,1,0:T(8,128)(2,1)S(1)} %fusion.5) | copy-start | bytes 14211076
  75.4 7.9 %copy-start.6 = (s32[8,2]{0,1:T(2,128)S(1)}, s32[8,2]{0,1:T(2,128)}, u32[]{:S(2)}) copy-start(s32[8,2]{0,1:T(2,128)} %param.10) | copy-start | bytes 196
  75.4 7.9 %copy-start.5 = (s32[8,1]{0,1:T(1,128)S(1)}, s32[8,1]{0,1:T(1,128)}, u32[]{:S(2)}) copy-start(s32[8,1]{0,1:T(1,128)} %param.11) | copy-start | bytes 100
  75.4 8.1 %copy-start.8 = (s32[8]{0:T(128)S(1)}, s32[8]{0:T(128)}, u32[]{:S(2)}) copy-start(s32[8]{0:T(128)} %param.13) | copy-start | bytes 100
  79.8 46.1 %collective-permute-start.2 = (bf16[15,512,256]{2,1,0:T(8,128)(2,1)}, bf16[15,512,256]{2,1,0:T(8,128)(2,1)}, u32[]{:S(2)}, u32[]{:S(2)}) collective-permute-start(bf16[15,512,256]{2,1,0:T(8,128)(2,1)} %slice.230), channel_id=1, source_target_pairs={{1,0},{2,1},{3,2},{4,3},{5,4},{6,5},{7,6},{8,7},{9,8},{10,9},{11,1... | collective-permute-start | bytes 11796488 | tf_op jit(solution)/shard_map/ppermute | solution.py:31
  133.2 52.0 %copy-start.7 = (bf16[15,256]{1,0:T(8,128)(2,1)S(1)}, bf16[15,256]{1,0:T(8,128)(2,1)}, u32[]{:S(2)}) copy-start(bf16[15,256]{1,0:T(8,128)(2,1)} %param.17) | copy-start | bytes 23044
  157.6 30.0 %copy-start.4 = (bf16[2304,256]{1,0:T(8,128)(2,1)S(1)}, bf16[2304,256]{1,0:T(8,128)(2,1)}, u32[]{:S(2)}) copy-start(bf16[2304,256]{1,0:T(8,128)(2,1)} %param.15) | copy-start | bytes 3538948
  159.5 25.9 %collective-permute-start.3 = (bf16[2,16,16,256]{3,0,2,1:T(2,128)(2,1)S(1)}, bf16[2,16,16,256]{3,0,2,1:T(2,128)(2,1)S(1)}, u32[]{:S(2)}, u32[]{:S(2)}) collective-permute-start(bf16[2,16,16,256]{3,0,2,1:T(2,128)(2,1)S(1)} %get-tuple-element.28), channel_id=1, source_target_pairs={{31,0},{0,1},{1,2},{2,3},{3,4},{4,5},{5,6},{6,7},{7,8},{8,9},{9,10... | collective-permute-start | bytes 786440 | tf_op jit(solution)/shard_map/ppermute | solution.py:37
  159.6 25.9 %collective-permute-start.4 = (bf16[2,16,16,256]{3,0,2,1:T(2,128)(2,1)S(1)}, bf16[2,16,16,256]{3,0,2,1:T(2,128)(2,1)S(1)}, u32[]{:S(2)}, u32[]{:S(2)}) collective-permute-start(bf16[2,16,16,256]{3,0,2,1:T(2,128)(2,1)S(1)} %get-tuple-element.27), channel_id=1, source_target_pairs={{30,0},{31,1},{0,2},{1,3},{2,4},{3,5},{4,6},{5,7},{6,8},{7,9},{8,1... | collective-permute-start | bytes 786440 | tf_op jit(solution)/shard_map/ppermute | solution.py:37
  161.2 24.3 %collective-permute-start.5 = (bf16[2,16,16,256]{3,0,2,1:T(2,128)(2,1)S(1)}, bf16[2,16,16,256]{3,0,2,1:T(2,128)(2,1)S(1)}, u32[]{:S(2)}, u32[]{:S(2)}) collective-permute-start(bf16[2,16,16,256]{3,0,2,1:T(2,128)(2,1)S(1)} %get-tuple-element.26), channel_id=1, source_target_pairs={{29,0},{30,1},{31,2},{0,3},{1,4},{2,5},{3,6},{4,7},{5,8},{6,9},{7,... | collective-permute-start | bytes 786440 | tf_op jit(solution)/shard_map/ppermute | solution.py:37
  161.3 20.0 %collective-permute-start.6 = (s32[2]{0:T(128)S(1)}, s32[2]{0:T(128)S(1)}, u32[]{:S(2)}, u32[]{:S(2)}) collective-permute-start(s32[2]{0:T(128)S(1)} %get-tuple-element.34), channel_id=1, source_target_pairs={{31,0},{0,1},{1,2},{2,3},{3,4},{4,5},{5,6},{6,7},{7,8},{8,9},{9,10... | collective-permute-start | bytes 32 | tf_op jit(solution)/shard_map/ppermute | solution.py:37
  164.5 16.7 %collective-permute-start.7 = (s32[2]{0:T(128)S(1)}, s32[2]{0:T(128)S(1)}, u32[]{:S(2)}, u32[]{:S(2)}) collective-permute-start(s32[2]{0:T(128)S(1)} %get-tuple-element.33), channel_id=1, source_target_pairs={{30,0},{31,1},{0,2},{1,3},{2,4},{3,5},{4,6},{5,7},{6,8},{7,9},{8,1... | collective-permute-start | bytes 32 | tf_op jit(solution)/shard_map/ppermute | solution.py:37
  181.3 3.9 %collective-permute-start.8 = (s32[2]{0:T(128)S(1)}, s32[2]{0:T(128)S(1)}, u32[]{:S(2)}, u32[]{:S(2)}) collective-permute-start(s32[2]{0:T(128)S(1)} %get-tuple-element.32), channel_id=1, source_target_pairs={{29,0},{30,1},{31,2},{0,3},{1,4},{2,5},{3,6},{4,7},{5,8},{6,9},{7,... | collective-permute-start | bytes 32 | tf_op jit(solution)/shard_map/ppermute | solution.py:37
where the time goes:
time: 228 us; the launch traced here: 227 us
  matrix products  94.9 us (42%)
  waiting for transfers between devices  62.2 us (27%)
  local copies, waits for them, and re-layouts  40.3 us (18%)
  starting transfers between devices  16.1 us (7%)
  other arithmetic  12.5 us (5%)
    dot_general x17, matrix products, conv_taps(): jnp.einsum('...c,cd->...d', window, piece, preferred_element_type=jnp.flo...  77.9 us
    ppermute x1, waiting for transfers between devices, passed_along(): return lax.ppermute(x, axis, pairs)  42.3 us
    gather x24, local copies, waits for them, and re-layouts  24.3 us
    ppermute x6, waiting for transfers between devices, passed_along_2(): return lax.ppermute(block, axis, route)  19.9 us
    dot_general x1, matrix products, mask_head(): jnp.einsum('bhwc,ck->bhwk', hidden, deconv_weight, preferred_element_type...  8.99 us
    reshape x1, local copies, waits for them, and re-layouts, mask_head(): jax.nn.relu(upsampled).astype(jnp.bfloat16)  7.84 us
    concatenate x1, other arithmetic, body(): stacked = jnp.concatenate([fpn_band, below], 0)  7.29 us
    dot_general x1, matrix products, mask_head(): jnp.einsum('bhwyxc,bc->bhwyx', upsampled, chosen, preferred_element_type=...  7.16 us
  transfers between devices with their start and end apart: 9, of which 3 were waited for; matrix products, arithmetic and copies ran while one was open for 3% of the time, Pallas kernels for 0%

commit v1 on v0

v1 whole, which is shorter than its diff:
```python
import functools

import jax
import jax.numpy as jnp
from jax import lax
from jax.experimental import pallas as pl
from jax.experimental.pallas import tpu as pltpu
from jax.sharding import PartitionSpec as P

SIDE = 16
WINDOW = 4
SLOTS = 2
EDGE = 16
GROUP = 2
MESH = pl.DeviceIdType.MESH


def kernel(
    count,
    meta_sm,
    meta_vm,
    feat,
    fpn_hbm,
    head_hbm,
    dec_hbm,
    cls_w,
    out,
    band,
    wide,
    fpn_w,
    head_w,
    dec_w,
    above_row,
    near_vm,
    near_sm,
    sent,
    got,
    ends,
    joined,
    wins,
    blocks,
    logits,
    outgoing,
    incoming,
    load_sem,
    small_send,
    small_recv,
    piece_send,
    piece_recv,
    mask_send,
    mask_recv,
):
    me = lax.axis_index("rows")
    rois = sent.shape[0]
    band_rows, columns, chans = band.shape
    has_up = me > 0
    has_down = me < count - 1

    def at(step):
        return {"rows": lax.rem(me + step + count, count)}

    barrier = pltpu.get_barrier_semaphore()
    for step in range(1, WINDOW):
        for sign in (1, -1):
            pl.semaphore_signal(barrier, inc=1, device_id=at(sign * step), device_id_type=MESH)

    loads = [
        pltpu.make_async_copy(feat, band, load_sem.at[0]),
        pltpu.make_async_copy(fpn_hbm, fpn_w, load_sem.at[1]),
        pltpu.make_async_copy(head_hbm, head_w, load_sem.at[2]),
        pltpu.make_async_copy(dec_hbm, dec_w, load_sem.at[3]),
    ]
    for load in loads:
        load.start()

    halves = wide.shape[0]
    lanes = wide.shape[-1]
    wide[:, :, 0:EDGE, :] = jnp.zeros((halves, band_rows + 1, EDGE, lanes), jnp.float32)
    wide[:, :, EDGE + columns :, :] = jnp.zeros((halves, band_rows + 1, EDGE, lanes), jnp.float32)
    blocks[...] = jnp.zeros_like(blocks)

    pl.semaphore_wait(barrier, 2 * (WINDOW - 1))

    corners_up = pltpu.make_async_remote_copy(
        src_ref=meta_vm,
        dst_ref=near_vm,
        send_sem=small_send.at[0],
        recv_sem=small_recv.at[0],
        device_id=at(1),
        device_id_type=MESH,
    )
    last_row = pltpu.make_async_remote_copy(
        src_ref=band.at[pl.ds(band_rows - 1, 1)],
        dst_ref=above_row,
        send_sem=small_send.at[1],
        recv_sem=small_recv.at[1],
        device_id=at(1),
        device_id_type=MESH,
    )

    @pl.when(has_down)
    def _():
        corners_up.start()

    loads[0].wait()

    @pl.when(has_down)
    def _():
        last_row.start()

    def widen(i, carry):
        for h in range(halves):
            wide[h, pl.ds(i + 1, 1), EDGE : EDGE + columns, :] = band[
                pl.ds(i, 1), :, h * lanes : (h + 1) * lanes
            ].astype(jnp.float32)
        return carry

    lax.fori_loop(0, band_rows, widen, 0)

    def piece(q):
        return pltpu.make_async_remote_copy(
            src_ref=sent.at[q],
            dst_ref=got.at[q],
            send_sem=piece_send.at[q],
            recv_sem=piece_recv.at[q],
            device_id=at(-1),
            device_id_type=MESH,
        )

    @pl.when(has_up)
    def _():
        corners_up.wait_recv()
        near = pltpu.make_async_copy(near_vm, near_sm, load_sem.at[4])
        near.start()
        near.wait()

        def gather(q, carry):
            start = near_sm[q, 1] + (EDGE - 1)
            for h in range(halves):
                part = slice(h * lanes, (h + 1) * lanes)
                for i in range(band_rows):
                    sent[q, i, :, part] = wide[h, i + 1, pl.ds(start + 1, SIDE), :].astype(
                        jnp.bfloat16
                    )
                    ends[0, i : i + 1, part] = wide[h, i + 1, pl.ds(start, 1), :]
                    ends[1, i : i + 1, part] = wide[h, i + 1, pl.ds(start + SIDE + 1, 1), :]
            sent[q, SIDE:] = ends[...].astype(jnp.bfloat16)
            piece(q).start()
            return carry

        lax.fori_loop(0, rois, gather, 0)
        last_row.wait_recv()
        for h in range(halves):
            wide[h, 0:1, EDGE : EDGE + columns, :] = above_row[
                :, :, h * lanes : (h + 1) * lanes
            ].astype(jnp.float32)

    @pl.when(jnp.logical_not(has_up))
    def _():
        wide[:, 0:1, EDGE : EDGE + columns, :] = jnp.zeros((halves, 1, columns, lanes), jnp.float32)

    def own(q, carry):
        start = meta_sm[q, 1] + (EDGE - 1)
        for dj in range(3):
            for h in range(halves):
                for i in range(band_rows + 1):
                    wins[q, dj, i, :, h * lanes : (h + 1) * lanes] = wide[
                        h, i, pl.ds(start + dj, SIDE), :
                    ].astype(jnp.bfloat16)
        return carry

    lax.fori_loop(0, rois, own, 0)

    @pl.when(jnp.logical_not(has_down))
    def _():
        got[...] = jnp.zeros_like(got)

    for load in loads[1:]:
        load.wait()

    limit = jnp.where(has_down, 2 * band_rows, band_rows)

    def group(g, carry):
        base = g * GROUP
        for u in range(GROUP):
            q = base + u

            @pl.when(has_down)
            def _():
                piece(q).wait_recv()

            joined[:, 8 : 8 + SIDE, :] = got[q, 0:SIDE].astype(jnp.float32)
            ends[...] = got[q, SIDE:].astype(jnp.float32)
            for i in range(band_rows):
                joined[i, 7:8, :] = ends[0, i : i + 1, :]
                joined[i, 8 + SIDE : 9 + SIDE, :] = ends[1, i : i + 1, :]
            for dj in range(3):
                wins[q, dj, band_rows + 1 :] = joined[:, 7 + dj : 7 + dj + SIDE, :].astype(
                    jnp.bfloat16
                )
        tops = [lax.rem(meta_sm[base + u, 0], band_rows) for u in range(GROUP)]
        total = None
        for tap in range(9):
            di, dj = tap // 3, tap % 3
            lhs = jnp.concatenate(
                [
                    wins[base + u, dj, pl.ds(tops[u] + di, SIDE)].reshape(SIDE * SIDE, chans)
                    for u in range(GROUP)
                ],
                axis=0,
            )
            term = jnp.dot(
                lhs, fpn_w[tap * chans : (tap + 1) * chans], preferred_element_type=jnp.float32
            )
            total = term if total is None else total + term
        total = total.reshape(GROUP, SIDE, SIDE, chans)
        row = lax.broadcasted_iota(jnp.int32, (SIDE, SIDE, chans), 0)
        for u in range(GROUP):
            kept = jnp.where(row + tops[u] < limit, total[u], 0.0)
            blocks[u, 1 : 1 + SIDE, 8 : 8 + SIDE, :] = kept
        total = None
        for tap in range(9):
            di, dj = tap // 3, tap % 3
            lhs = (
                blocks[:, di : di + SIDE, 7 + dj : 7 + dj + SIDE, :]
                .astype(jnp.bfloat16)
                .reshape(GROUP * SIDE * SIDE, chans)
            )
            term = jnp.dot(
                lhs, head_w[tap * chans : (tap + 1) * chans], preferred_element_type=jnp.float32
            )
            total = term if total is None else total + term
        hidden = jnp.maximum(total, 0.0).astype(jnp.bfloat16)
        for yx in range(4):
            up = jnp.dot(
                hidden, dec_w[:, yx * chans : (yx + 1) * chans], preferred_element_type=jnp.float32
            )
            up = jnp.maximum(up, 0.0).astype(jnp.bfloat16)
            every = lax.dot_general(
                cls_w[...], up, (((1,), (1,)), ((), ())), preferred_element_type=jnp.float32
            )
            which = lax.broadcasted_iota(jnp.int32, (every.shape[0], SIDE * SIDE), 0)
            for u in range(GROUP):
                mine = every[:, u * SIDE * SIDE : (u + 1) * SIDE * SIDE]
                logits[base + u, yx : yx + 1, :] = jnp.sum(
                    jnp.where(which == meta_sm[base + u, 3], mine, 0.0), axis=0, keepdims=True
                )
        return carry

    lax.fori_loop(0, rois // GROUP, group, 0)

    slots = []
    for q in range(rois):
        rank = jnp.int32(0)
        for p in range(q):
            same = (meta_sm[p, 2] == meta_sm[q, 2]) & (p < meta_sm[p, 4])
            rank = rank + same.astype(jnp.int32)
        slots.append(jnp.where(q < meta_sm[q, 4], meta_sm[q, 2] * SLOTS + rank, WINDOW * SLOTS))

    def mask(f):
        return pltpu.make_async_remote_copy(
            src_ref=outgoing.at[f],
            dst_ref=incoming.at[f],
            send_sem=mask_send.at[f],
            recv_sem=mask_recv.at[f],
            device_id=at(f),
            device_id_type=MESH,
        )

    for f in range(WINDOW - 1, -1, -1):
        for k in range(SLOTS):
            held = jnp.zeros(logits.shape[1:], jnp.float32)
            for q in range(rois):
                held = jnp.where(slots[q] == f * SLOTS + k, logits[q], held)
            if f:
                outgoing[f, k] = held
            else:
                out[k] = held
        if f:
            mask(f).start()

    for f in range(1, WINDOW):
        mask(f).wait_recv()
        out[f * SLOTS : (f + 1) * SLOTS] = incoming[f]

    for f in range(1, WINDOW):
        mask(f).wait_send()

    @pl.when(has_down)
    def _():
        corners_up.wait_send()
        last_row.wait_send()

    @pl.when(has_up)
    def _():
        def drain(q, carry):
            piece(q).wait_send()
            return carry

        lax.fori_loop(0, rois, drain, 0)


def body(
    count,
    features,
    corners,
    offsets,
    counts,
    classes,
    fpn_weight,
    head_weight,
    deconv_weight,
    class_weight,
):
    band_rows, columns, chans = features.shape
    rois = corners.shape[0]
    meta = jnp.concatenate(
        [corners, offsets, classes[:, None], jnp.broadcast_to(counts[:, None], (rois, 1))], 1
    )
    meta = jnp.pad(meta, ((0, 0), (0, 128 - meta.shape[1])))
    cls = class_weight
    vmem = pl.BlockSpec(memory_space=pltpu.VMEM)
    anyw = pl.BlockSpec(memory_space=pl.ANY)
    bf16, f32 = jnp.bfloat16, jnp.float32
    cells = SIDE * SIDE
    masks = pl.pallas_call(
        functools.partial(kernel, count),
        out_shape=jax.ShapeDtypeStruct((WINDOW * SLOTS, 4, cells), f32),
        in_specs=[pl.BlockSpec(memory_space=pltpu.SMEM), vmem, anyw, anyw, anyw, anyw, vmem],
        out_specs=vmem,
        scratch_shapes=[
            pltpu.VMEM(features.shape, bf16),
            pltpu.VMEM((chans // 128, band_rows + 1, columns + 2 * EDGE, 128), f32),
            pltpu.VMEM(fpn_weight.shape, bf16),
            pltpu.VMEM(head_weight.shape, bf16),
            pltpu.VMEM(deconv_weight.shape, bf16),
            pltpu.VMEM((1, columns, chans), bf16),
            pltpu.VMEM((rois, 128), jnp.int32),
            pltpu.SMEM((rois, 128), jnp.int32),
            pltpu.VMEM((rois, SIDE + 2, SIDE, chans), bf16),
            pltpu.VMEM((rois, SIDE + 2, SIDE, chans), bf16),
            pltpu.VMEM((2, SIDE, chans), f32),
            pltpu.VMEM((SIDE, 2 * SIDE, chans), f32),
            pltpu.VMEM((rois, 3, 2 * band_rows + 1, SIDE, chans), bf16),
            pltpu.VMEM((GROUP, SIDE + 2, 2 * SIDE, chans), f32),
            pltpu.VMEM((rois, 4, cells), f32),
            pltpu.VMEM((WINDOW, SLOTS, 4, cells), f32),
            pltpu.VMEM((WINDOW, SLOTS, 4, cells), f32),
            pltpu.SemaphoreType.DMA((5,)),
            pltpu.SemaphoreType.DMA((2,)),
            pltpu.SemaphoreType.DMA((2,)),
            pltpu.SemaphoreType.DMA((rois,)),
            pltpu.SemaphoreType.DMA((rois,)),
            pltpu.SemaphoreType.DMA((WINDOW,)),
            pltpu.SemaphoreType.DMA((WINDOW,)),
        ],
        compiler_params=pltpu.CompilerParams(collective_id=0, has_side_effects=True),
    )(meta, meta, features, fpn_weight, head_weight, deconv_weight, cls)
    masks = masks.reshape(WINDOW * SLOTS, 2, 2, SIDE, SIDE)
    return masks.transpose(0, 3, 1, 4, 2).reshape(WINDOW * SLOTS, 4 * cells)


def solution(mesh):
    placed = (
        P(("tiles", "rows"), None, None),
        P(("tiles", "rows"), None),
        P(("tiles", "rows"), None),
        P(("tiles", "rows")),
        P(("tiles", "rows")),
        P(),
        P(),
        P(),
        P(),
    )
    return jax.shard_map(
        functools.partial(body, mesh.shape["rows"]),
        mesh=mesh,
        in_specs=placed,
        out_specs=P(("tiles", "rows"), None),
        check_vma=False,
    )
```

time: 228 us -> 49.6 us (0.22)
  the two profiles are of different devices: /device:TPU:8 before, /device:TPU:4 now
where the time goes in v1:
time: 49.6 us; the launch traced here: 49.3 us
  Pallas kernels  43.7 us (88%)
  local copies, waits for them, and re-layouts  4.87 us (10%)
  between operations  0.67 us (1%)
    pallas_call x1, Pallas kernels, body(): pl.pallas_call(functools.partial(kernel, count), out_shape=jax.ShapeDtype...  43.7 us
    unnamed x2, local copies, waits for them, and re-layouts  1.48 us
    reshape x2, local copies, waits for them, and re-layouts, body(): masks = masks.reshape(WINDOW * SLOTS, 2, 2, SIDE, SIDE)  1.19 us

profile of v1, /device:TPU:4, one launch (start us, length us, event | category | flops | bytes accessed | tf_op | source)
XLA Modules:
  0.0 49.3 jit_solution(14633723949186310119)
XLA Ops:
  0.7 0.1 pad.8.clone
  0.7 0.8 %copy.14 = s32[8,2]{1,0:T(8,128)S(1)} copy(s32[8,2]{0,1:T(2,128)} %param.10) | data formatting | bytes 128 | tf_op args[1]
  1.5 0.7 %copy.15 = s32[8,1]{1,0:T(8,128)S(1)} copy(s32[8,1]{0,1:T(1,128)} %param.11) | data formatting | bytes 64 | tf_op args[2]
  2.2 0.7 %copy.16 = s32[8,1]{1,0:T(8,128)S(1)} copy(s32[8,1]{0,1:T(1,128)} %bitcast.6) | data formatting | bytes 64 | tf_op jit(solution)/shard_map/broadcast_in_dim | solution.py:318
  2.9 0.1 add_add_fusion
  3.0 0.6 %pad.4.meta_sm.meta_vm = s32[8,128]{1,0:T(8,128)} pad(s32[8,5]{1,0:T(8,128)S(1)} %add_add_fusion, s32[]{:T(128)} %constant.0.clone.1), padding=0_0x0_123 | pad | bytes 4260 | tf_op jit(solution)/shard_map/jit(_pad)/pad | solution.py:320
  3.6 43.7 %shard_map.91 = f32[8,4,256]{2,1,0:T(4,128)} custom-call(s32[8,128]{1,0:T(8,128)} %pad.4.meta_sm.meta_vm, s32[8,128]{1,0:T(8,128)} %pad.4.meta_sm.meta_vm, bf16[16,512,256]{2,1,0:T(8,128)(2,1)} %feat.1, bf16[2304,256]{1,0:T(8,128)(2,1)} %fpn_hbm.1, bf16[2304,256]{1,0:T(8,128)(2,1)} %head_hbm.1, bf16[256,1024]{1,0:T(8,128)(2,1)} %dec_hbm.1, bf16[15,256]{1,0:T(8,128)(2,1)} %cls_w.1), custom_call_target="tpu_custom_call" | custom-call | tf_op jit(solution)/shard_map/pallas_call | solution.py:326
  47.3 0.9 %reshape.9 = f32[8,2,2,16,16]{4,3,2,1,0:T(8,128)S(1)} reshape(f32[8,4,256]{2,1,0:T(4,128)} %shard_map.91) | data formatting | bytes 65536 | tf_op jit(solution)/shard_map/reshape | solution.py:359
  48.2 0.3 copy.17
  48.5 0.8 %copy.18 = f32[8,1024]{1,0:T(8,128)} copy(f32[8,1024]{0,1:T(8,128)S(1)} %bitcast.5) | data formatting | bytes 65536 | tf_op jit(solution)/shard_map/reshape | solution.py:360

commit v2 on v1

--- a/solution.py
+++ b/solution.py
@@ -17,8 +17,11 @@
 
 def kernel(
     count,
-    meta_sm,
-    meta_vm,
+    corners_sm,
+    corners_vm,
+    offset_sm,
+    count_sm,
+    class_sm,
     feat,
     fpn_hbm,
     head_hbm,
@@ -82,7 +85,7 @@
     pl.semaphore_wait(barrier, 2 * (WINDOW - 1))
 
     corners_up = pltpu.make_async_remote_copy(
-        src_ref=meta_vm,
+        src_ref=corners_vm,
         dst_ref=near_vm,
         send_sem=small_send.at[0],
         recv_sem=small_recv.at[0],
@@ -90,7 +93,7 @@
         device_id_type=MESH,
     )
     last_row = pltpu.make_async_remote_copy(
-        src_ref=band.at[pl.ds(band_rows - 1, 1)],
+        src_ref=feat.at[pl.ds(band_rows - 1, 1)],
         dst_ref=above_row,
         send_sem=small_send.at[1],
         recv_sem=small_recv.at[1],
@@ -101,12 +104,9 @@
     @pl.when(has_down)
     def _():
         corners_up.start()
+        last_row.start()
 
     loads[0].wait()
-
-    @pl.when(has_down)
-    def _():
-        last_row.start()
 
     def widen(i, carry):
         for h in range(halves):
@@ -135,7 +135,7 @@
         near.wait()
 
         def gather(q, carry):
-            start = near_sm[q, 1] + (EDGE - 1)
+            start = near_sm[1, q] + (EDGE - 1)
             for h in range(halves):
                 part = slice(h * lanes, (h + 1) * lanes)
                 for i in range(band_rows):
@@ -160,7 +160,7 @@
         wide[:, 0:1, EDGE : EDGE + columns, :] = jnp.zeros((halves, 1, columns, lanes), jnp.float32)
 
     def own(q, carry):
-        start = meta_sm[q, 1] + (EDGE - 1)
+        start = corners_sm[1, q] + (EDGE - 1)
         for dj in range(3):
             for h in range(halves):
                 for i in range(band_rows + 1):
@@ -198,7 +198,7 @@
                 wins[q, dj, band_rows + 1 :] = joined[:, 7 + dj : 7 + dj + SIDE, :].astype(
                     jnp.bfloat16
                 )
-        tops = [lax.rem(meta_sm[base + u, 0], band_rows) for u in range(GROUP)]
+        tops = [lax.rem(corners_sm[0, base + u], band_rows) for u in range(GROUP)]
         total = None
         for tap in range(9):
             di, dj = tap // 3, tap % 3
@@ -243,7 +243,7 @@
             for u in range(GROUP):
                 mine = every[:, u * SIDE * SIDE : (u + 1) * SIDE * SIDE]
                 logits[base + u, yx : yx + 1, :] = jnp.sum(
-                    jnp.where(which == meta_sm[base + u, 3], mine, 0.0), axis=0, keepdims=True
+                    jnp.where(which == class_sm[base + u], mine, 0.0), axis=0, keepdims=True
                 )
         return carry
 
@@ -253,9 +253,9 @@
     for q in range(rois):
         rank = jnp.int32(0)
         for p in range(q):
-            same = (meta_sm[p, 2] == meta_sm[q, 2]) & (p < meta_sm[p, 4])
+            same = (offset_sm[p] == offset_sm[q]) & (p < count_sm[0])
             rank = rank + same.astype(jnp.int32)
-        slots.append(jnp.where(q < meta_sm[q, 4], meta_sm[q, 2] * SLOTS + rank, WINDOW * SLOTS))
+        slots.append(jnp.where(q < count_sm[0], offset_sm[q] * SLOTS + rank, WINDOW * SLOTS))
 
     def mask(f):
         return pltpu.make_async_remote_copy(
@@ -314,10 +314,8 @@
 ):
     band_rows, columns, chans = features.shape
     rois = corners.shape[0]
-    meta = jnp.concatenate(
-        [corners, offsets, classes[:, None], jnp.broadcast_to(counts[:, None], (rois, 1))], 1
-    )
-    meta = jnp.pad(meta, ((0, 0), (0, 128 - meta.shape[1])))
+    spots = corners.T
+    smem = pl.BlockSpec(memory_space=pltpu.SMEM)
     cls = class_weight
     vmem = pl.BlockSpec(memory_space=pltpu.VMEM)
     anyw = pl.BlockSpec(memory_space=pl.ANY)
@@ -326,7 +324,7 @@
     masks = pl.pallas_call(
         functools.partial(kernel, count),
         out_shape=jax.ShapeDtypeStruct((WINDOW * SLOTS, 4, cells), f32),
-        in_specs=[pl.BlockSpec(memory_space=pltpu.SMEM), vmem, anyw, anyw, anyw, anyw, vmem],
+        in_specs=[smem, vmem, smem, smem, smem, anyw, anyw, anyw, anyw, vmem],
         out_specs=vmem,
         scratch_shapes=[
             pltpu.VMEM(features.shape, bf16),
@@ -335,8 +333,8 @@
             pltpu.VMEM(head_weight.shape, bf16),
             pltpu.VMEM(deconv_weight.shape, bf16),
             pltpu.VMEM((1, columns, chans), bf16),
-            pltpu.VMEM((rois, 128), jnp.int32),
-            pltpu.SMEM((rois, 128), jnp.int32),
+            pltpu.VMEM(spots.shape, jnp.int32),
+            pltpu.SMEM(spots.shape, jnp.int32),
             pltpu.VMEM((rois, SIDE + 2, SIDE, chans), bf16),
             pltpu.VMEM((rois, SIDE + 2, SIDE, chans), bf16),
             pltpu.VMEM((2, SIDE, chans), f32),
@@ -355,7 +353,18 @@
             pltpu.SemaphoreType.DMA((WINDOW,)),
         ],
         compiler_params=pltpu.CompilerParams(collective_id=0, has_side_effects=True),
-    )(meta, meta, features, fpn_weight, head_weight, deconv_weight, cls)
+    )(
+        spots,
+        spots,
+        offsets.reshape(rois),
+        counts,
+        classes,
+        features,
+        fpn_weight,
+        head_weight,
+        deconv_weight,
+        cls,
+    )
     masks = masks.reshape(WINDOW * SLOTS, 2, 2, SIDE, SIDE)
     return masks.transpose(0, 3, 1, 4, 2).reshape(WINDOW * SLOTS, 4 * cells)
 

time: 49.6 us -> 46.9 us (0.946)
  local copies, waits for them, and re-layouts: 4.87 us -> 1.98 us
    unnamed x2 -> x0, local copies, waits for them, and re-layouts: 1.48 us -> none
    broadcast_in_dim x1 -> x0, local copies, waits for them, and re-layouts: 0.73 us -> none  [body(): classes[:, None]]
    pad x1 -> x0, local copies, waits for them, and re-layouts: 0.6 us -> none  [body(): meta = jnp.pad(meta, ((0, 0), (0, 128 - meta.shape[1])))]
where the time goes in v2:
time: 46.9 us; the launch traced here: 46.6 us
  Pallas kernels  44 us (94%)
  local copies, waits for them, and re-layouts  1.98 us (4%)
  between operations  0.67 us (1%)
    pallas_call x1, Pallas kernels, body(): pl.pallas_call(functools.partial(kernel, count), out_shape=jax.ShapeDtype...  44 us
    reshape x2, local copies, waits for them, and re-layouts, body(): masks = masks.reshape(WINDOW * SLOTS, 2, 2, SIDE, SIDE)  1.19 us

profile of v2, /device:TPU:4, one launch (start us, length us, event | category | flops | bytes accessed | tf_op | source)
XLA Modules:
  0.0 46.6 jit_solution(12764556657722770176)
XLA Ops:
  0.7 44.0 %shard_map.91 = f32[8,4,256]{2,1,0:T(4,128)} custom-call(s32[2,8]{1,0:T(2,128)} %bitcast.6, s32[2,8]{1,0:T(2,128)} %bitcast.7, s32[8]{0:T(128)} %bitcast.8, s32[1]{0:T(128)S(6)} %copy.13.count_sm, s32[8]{0:T(128)} %class_sm.1, bf16[16,512,256]{2,1,0:T(8,128)(2,1)} %feat.1, bf16[2304,256]{1,0:T(8,128)(2,1)} %fpn_hbm.1, bf16[2304,256]{1,0:T(8,128)(2,1)} %head_hbm.1, ...), custom_call_target="tpu_custom_call" | custom-call | tf_op jit(solution)/shard_map/pallas_call | solution.py:324
  44.6 0.9 %reshape.10 = f32[8,2,2,16,16]{4,3,2,1,0:T(8,128)S(1)} reshape(f32[8,4,256]{2,1,0:T(4,128)} %shard_map.91) | data formatting | bytes 65536 | tf_op jit(solution)/shard_map/reshape | solution.py:368
  45.5 0.3 copy.11
  45.8 0.8 %copy.12 = f32[8,1024]{1,0:T(8,128)} copy(f32[8,1024]{0,1:T(8,128)S(1)} %bitcast.5) | data formatting | bytes 65536 | tf_op jit(solution)/shard_map/reshape | solution.py:369

commit v3 on v2

--- a/solution.py
+++ b/solution.py
@@ -129,6 +129,11 @@
 
     @pl.when(has_up)
     def _():
+        last_row.wait_recv()
+        for h in range(halves):
+            wide[h, 0:1, EDGE : EDGE + columns, :] = above_row[
+                :, :, h * lanes : (h + 1) * lanes
+            ].astype(jnp.float32)
         corners_up.wait_recv()
         near = pltpu.make_async_copy(near_vm, near_sm, load_sem.at[4])
         near.start()
@@ -149,11 +154,6 @@
             return carry
 
         lax.fori_loop(0, rois, gather, 0)
-        last_row.wait_recv()
-        for h in range(halves):
-            wide[h, 0:1, EDGE : EDGE + columns, :] = above_row[
-                :, :, h * lanes : (h + 1) * lanes
-            ].astype(jnp.float32)
 
     @pl.when(jnp.logical_not(has_up))
     def _():

time: 46.9 us -> 39.9 us (0.85)
  the two profiles are of different devices: /device:TPU:4 before, /device:TPU:0 now
where the time goes in v3:
time: 39.9 us; the launch traced here: 39.7 us
  Pallas kernels  37 us (93%)
  local copies, waits for them, and re-layouts  1.98 us (5%)
  between operations  0.67 us (2%)
    pallas_call x1, Pallas kernels, body(): pl.pallas_call(functools.partial(kernel, count), out_shape=jax.ShapeDtype...  37 us
    reshape x2, local copies, waits for them, and re-layouts, body(): masks = masks.reshape(WINDOW * SLOTS, 2, 2, SIDE, SIDE)  1.19 us

profile of v3, /device:TPU:0, one launch (start us, length us, event | category | flops | bytes accessed | tf_op | source)
XLA Modules:
  0.0 39.7 jit_solution(15545560380125947252)
XLA Ops:
  0.7 37.0 %shard_map.91 = f32[8,4,256]{2,1,0:T(4,128)} custom-call(s32[2,8]{1,0:T(2,128)} %bitcast.6, s32[2,8]{1,0:T(2,128)} %bitcast.7, s32[8]{0:T(128)} %bitcast.8, s32[1]{0:T(128)S(6)} %copy.13.count_sm, s32[8]{0:T(128)} %class_sm.1, bf16[16,512,256]{2,1,0:T(8,128)(2,1)} %feat.1, bf16[2304,256]{1,0:T(8,128)(2,1)} %fpn_hbm.1, bf16[2304,256]{1,0:T(8,128)(2,1)} %head_hbm.1, ...), custom_call_target="tpu_custom_call" | custom-call | tf_op jit(solution)/shard_map/pallas_call | solution.py:324
  37.7 0.9 %reshape.10 = f32[8,2,2,16,16]{4,3,2,1,0:T(8,128)S(1)} reshape(f32[8,4,256]{2,1,0:T(4,128)} %shard_map.91) | data formatting | bytes 65536 | tf_op jit(solution)/shard_map/reshape | solution.py:368
  38.6 0.3 copy.11
  38.9 0.8 %copy.12 = f32[8,1024]{1,0:T(8,128)} copy(f32[8,1024]{0,1:T(8,128)S(1)} %bitcast.5) | data formatting | bytes 65536 | tf_op jit(solution)/shard_map/reshape | solution.py:369
